TPU v7x, 32 devices: a whole 2x2x4 slice. The times are simulated.
32 devices in a mesh: kpt: 8 (over z, core), row: 4 (over y, x).
Axes of the slice: x: 2, y: 2, z: 4, core: 2. Of those that a mesh axis runs over, the one named last changes fastest.
Arguments:
- occ_orbitals: bfloat16 [32, 2048, 128], P('kpt', 'row'), may hold values from -0.5 to 0.5
- virt_orbitals: bfloat16 [32, 2048, 256], P('kpt', 'row'), may hold values from -0.375 to 0.375
- occ_gap: bfloat16 [32, 128], P('kpt'), may hold values from 0.049804688 to 3
- virt_gap: bfloat16 [32, 256], P('kpt'), may hold values from 0.049804688 to 3
- partner: int32 [3, 32], replicated, may hold values from 0 to 31, as said below
Outputs:
- chi: float32 [3, 4, 2048, 2048], P(None, None, 'row', 'kpt')
Inputs may be any that keep to these rules, and one draw needn't show every extreme that they name: For each transfer q there is a shift s_q of 0 to 4 with partner[q, k] = (k - s_q) mod 32 for every k; the shifts of different transfers differ, and some transfer has s_q = 4.
All inputs are finite; a program needn't handle non-finite values.
Results may differ from a plain program's by a relative error of at most 0.0003.
Values may be sent and summed in bfloat16 or wider, within the bound.
A program may use at most 384 MiB of HBM per device.

v0:
```python
import jax
import jax.numpy as jnp
from jax import lax
from jax.sharding import PartitionSpec as P

NTAU = 4


def weighted(orbitals, energy_gap, moment):
    factor = jnp.exp(-energy_gap.astype(jnp.float32) * moment)
    return (orbitals.astype(jnp.float32) * factor[:, None, :]).astype(jnp.bfloat16)


def greens(row_panel, column_panel):
    return jnp.einsum("kri,kci->krc", row_panel, column_panel, preferred_element_type=jnp.float32)


def on_device(occ_orbitals, virt_orbitals, occ_gap, virt_gap, partner):
    transfers = partner.shape[0]
    tau_values = 0.25 * 2.0 ** jnp.arange(NTAU, dtype=jnp.float32)
    occ_points, virt_points = (
        lax.all_gather(occ_orbitals, "row", axis=1, tiled=True),
        lax.all_gather(virt_orbitals, "row", axis=1, tiled=True),
    )
    occ_columns, virt_columns = (
        lax.all_to_all(occ_points, "kpt", split_axis=1, concat_axis=0, tiled=True),
        lax.all_to_all(virt_points, "kpt", split_axis=1, concat_axis=0, tiled=True),
    )
    occ_all, virt_all, occ_gaps, virt_gaps = (
        lax.all_gather(occ_orbitals, "kpt", axis=0, tiled=True),
        lax.all_gather(virt_orbitals, "kpt", axis=0, tiled=True),
        lax.all_gather(occ_gap, "kpt", axis=0, tiled=True),
        lax.all_gather(virt_gap, "kpt", axis=0, tiled=True),
    )
    blocks = []
    for step_index in range(NTAU):
        moment = tau_values[step_index]
        occ_green = greens(weighted(occ_all, occ_gaps, moment), occ_columns)
        every_green = greens(weighted(virt_all, virt_gaps, moment), virt_columns)
        sums_here = []
        for transfer in range(transfers):
            virt_green = jnp.take(every_green, partner[transfer], axis=0)
            sums_here.append(jnp.sum(occ_green * virt_green, axis=0))
        blocks.append(jnp.stack(sums_here))
    return jnp.stack(blocks, axis=1)


def solution(mesh):
    in_specs = (P("kpt", "row", None), P("kpt", "row", None), P("kpt", None), P("kpt", None), P())
    out_specs = P(None, None, "row", "kpt")
    return jax.shard_map(
        on_device, mesh=mesh, in_specs=in_specs, out_specs=out_specs, check_vma=False
    )
```

profile of v0, /device:TPU:26, one launch (start us, length us, event | category | flops | bytes accessed | tf_op | source)
XLA Modules:
  0.0 658.1 jit_solution(4570953317096927387)
XLA Ops:
  13.2 32.1 %all-gather.9.cloned.1.call-done = bf16[4,2048,128]{2,0,1:T(4,128)(2,1)} async-done(((bf16[4,512,128]{2,0,1:T(4,128)(2,1)}), bf16[4,2048,128]{2,0,1:T(4,128)(2,1)}) %all-gather.9.cloned.1.call-update) | async-done | bytes 2097168 | tf_op jit(solution)/shard_map/all_gather | solution.py:22
  50.4 49.3 %all-gather.13.cloned.1.call-done = bf16[4,2048,256]{2,0,1:T(4,128)(2,1)} async-done(((bf16[4,512,256]{2,0,1:T(4,128)(2,1)}), bf16[4,2048,256]{2,0,1:T(4,128)(2,1)}) %all-gather.13.cloned.1.call-update) | async-done | bytes 4194320 | tf_op jit(solution)/shard_map/all_gather | solution.py:23
  104.9 186.8 %all-gather.1 = bf16[8,4,256]{2,1,0:T(4,128)(2,1)S(1)} all-gather(bf16[1,4,256]{2,1,0:T(4,128)(2,1)S(1)} %bitcast.97), channel_id=1, replica_groups=mesh['kpt'=8,'row'=4] {'kpt'}, dimensions={0}, use_global_device_ids=true | all-gather | bytes 18432 | tf_op jit(solution)/shard_map/all_gather | solution.py:33
  295.0 8.4 %all-gather = bf16[8,4,128]{2,1,0:T(4,128)(2,1)S(1)} all-gather(bf16[1,4,128]{2,1,0:T(4,128)(2,1)S(1)} %bitcast.98), channel_id=1, replica_groups=mesh['kpt'=8,'row'=4] {'kpt'}, dimensions={0}, use_global_device_ids=true | all-gather | bytes 9216 | tf_op jit(solution)/shard_map/all_gather | solution.py:32
  309.3 10.4 %fusion.34 = f32[32,512,256]{2,1,0:T(8,128)} fusion(bf16[32,256,128]{2,1,0:T(8,128)(2,1)S(1)} %bitcast.70, bf16[32,512,128]{2,1,0:T(8,128)(2,1)} %all-gather.7.cloned.1.call-done, f32[32,128]{1,0:T(8,128)S(1)} %bitcast.94), kind=kOutput, calls=%fused_computation.62 | convolution fusion | flops 1080033280 | bytes 23085056 | tf_op jit(solution)/shard_map/kri,kci->krc/dot_general | solution.py:15
  319.7 8.1 %fusion.36 = f32[32,512,256]{2,1,0:T(8,128)} fusion(bf16[32,256,128]{2,1,0:T(8,128)(2,1)S(1)} %bitcast.71, bf16[32,512,128]{2,1,0:T(8,128)(2,1)S(1)} %copy-done, f32[32,128]{1,0:T(8,128)S(1)} %bitcast.93), kind=kOutput, calls=%fused_computation.63 | convolution fusion | flops 1080033280 | bytes 23085056 | tf_op jit(solution)/shard_map/kri,kci->krc/dot_general | solution.py:15
  327.8 8.1 %fusion.38 = f32[32,512,256]{2,1,0:T(8,128)} fusion(bf16[32,256,128]{2,1,0:T(8,128)(2,1)S(1)} %bitcast.72, bf16[32,512,128]{2,1,0:T(8,128)(2,1)S(1)} %copy-done, f32[32,128]{1,0:T(8,128)S(1)} %bitcast.92), kind=kOutput, calls=%fused_computation.64 | convolution fusion | flops 1080033280 | bytes 23085056 | tf_op jit(solution)/shard_map/kri,kci->krc/dot_general | solution.py:15
  340.8 12.8 %fusion.26 = f32[32,512,256]{2,1,0:T(8,128)} fusion(bf16[32,256,256]{2,1,0:T(8,128)(2,1)} %bitcast.66, bf16[32,512,256]{2,1,0:T(8,128)(2,1)} %all-gather.11.cloned.1.call-done, f32[32,256]{1,0:T(8,128)S(1)} %reshape.146), kind=kOutput, calls=%fused_computation.55 | convolution fusion | flops 2160066560 | bytes 29392896 | tf_op jit(solution)/shard_map/kri,kci->krc/dot_general | solution.py:15
  353.6 14.2 %gather_fusion.1 = f32[32,512,256]{2,1,0:T(8,128)} fusion(f32[32,512,256]{2,1,0:T(8,128)} %fusion.26, s32[1024]{0:T(1024)S(1)} %get-tuple-element.50), kind=kCustom, calls=%fused_computation.1.clone | custom fusion | bytes 33554560 | tf_op jit(solution)/shard_map/jit(_take)/gather | solution.py:42
  367.8 14.2 %gather_fusion.2 = f32[32,512,256]{2,1,0:T(8,128)} fusion(f32[32,512,256]{2,1,0:T(8,128)} %fusion.26, s32[1024]{0:T(1024)S(1)} %get-tuple-element.49), kind=kCustom, calls=%fused_computation.2.clone | custom fusion | bytes 33554560 | tf_op jit(solution)/shard_map/jit(_take)/gather | solution.py:42
  382.0 12.8 %fusion.24 = f32[32,512,256]{2,1,0:T(8,128)} fusion(bf16[32,256,256]{2,1,0:T(8,128)(2,1)} %bitcast.67, bf16[32,512,256]{2,1,0:T(8,128)(2,1)} %all-gather.11.cloned.1.call-done, f32[32,256]{1,0:T(8,128)S(1)} %reshape.148), kind=kOutput, calls=%fused_computation.54 | convolution fusion | flops 2160066560 | bytes 29392896 | tf_op jit(solution)/shard_map/kri,kci->krc/dot_general | solution.py:15
  394.7 14.2 %gather_fusion.4 = f32[32,512,256]{2,1,0:T(8,128)} fusion(f32[32,512,256]{2,1,0:T(8,128)} %fusion.24, s32[1024]{0:T(1024)S(1)} %get-tuple-element.50), kind=kCustom, calls=%fused_computation.4.clone | custom fusion | bytes 33554560 | tf_op jit(solution)/shard_map/jit(_take)/gather | solution.py:42
  408.9 14.1 %gather_fusion.5 = f32[32,512,256]{2,1,0:T(8,128)} fusion(f32[32,512,256]{2,1,0:T(8,128)} %fusion.24, s32[1024]{0:T(1024)S(1)} %get-tuple-element.49), kind=kCustom, calls=%fused_computation.5.clone | custom fusion | bytes 33554560 | tf_op jit(solution)/shard_map/jit(_take)/gather | solution.py:42
  423.0 12.7 %fusion.22 = f32[32,512,256]{2,1,0:T(8,128)} fusion(bf16[32,256,256]{2,1,0:T(8,128)(2,1)} %bitcast.68, bf16[32,512,256]{2,1,0:T(8,128)(2,1)} %all-gather.11.cloned.1.call-done, f32[32,256]{1,0:T(8,128)S(1)} %reshape.150), kind=kOutput, calls=%fused_computation.53 | convolution fusion | flops 2160066560 | bytes 29392896 | tf_op jit(solution)/shard_map/kri,kci->krc/dot_general | solution.py:15
  435.6 14.1 %gather_fusion.7 = f32[32,512,256]{2,1,0:T(8,128)} fusion(f32[32,512,256]{2,1,0:T(8,128)} %fusion.22, s32[1024]{0:T(1024)S(1)} %get-tuple-element.50), kind=kCustom, calls=%fused_computation.7.clone | custom fusion | bytes 33554560 | tf_op jit(solution)/shard_map/jit(_take)/gather | solution.py:42
  449.7 14.3 %gather_fusion.8 = f32[32,512,256]{2,1,0:T(8,128)} fusion(f32[32,512,256]{2,1,0:T(8,128)} %fusion.22, s32[1024]{0:T(1024)S(1)} %get-tuple-element.49), kind=kCustom, calls=%fused_computation.8.clone | custom fusion | bytes 33554560 | tf_op jit(solution)/shard_map/jit(_take)/gather | solution.py:42
  464.0 12.7 %fusion.20 = f32[32,512,256]{2,1,0:T(8,128)} fusion(bf16[32,256,256]{2,1,0:T(8,128)(2,1)} %bitcast.69, bf16[32,512,256]{2,1,0:T(8,128)(2,1)} %all-gather.11.cloned.1.call-done, f32[32,256]{1,0:T(8,128)S(1)} %reshape.152), kind=kOutput, calls=%fused_computation.52 | convolution fusion | flops 2160066560 | bytes 29392896 | tf_op jit(solution)/shard_map/kri,kci->krc/dot_general | solution.py:15
  476.7 14.1 %gather_fusion.10 = f32[32,512,256]{2,1,0:T(8,128)} fusion(f32[32,512,256]{2,1,0:T(8,128)} %fusion.20, s32[1024]{0:T(1024)S(1)} %get-tuple-element.50), kind=kCustom, calls=%fused_computation.10.clone | custom fusion | bytes 33554560 | tf_op jit(solution)/shard_map/jit(_take)/gather | solution.py:42
  490.7 14.1 %gather_fusion.11 = f32[32,512,256]{2,1,0:T(8,128)} fusion(f32[32,512,256]{2,1,0:T(8,128)} %fusion.20, s32[1024]{0:T(1024)S(1)} %get-tuple-element.49), kind=kCustom, calls=%fused_computation.11.clone | custom fusion | bytes 33554560 | tf_op jit(solution)/shard_map/jit(_take)/gather | solution.py:42
  504.8 14.1 %gather_fusion = f32[32,512,256]{2,1,0:T(8,128)} fusion(f32[32,512,256]{2,1,0:T(8,128)} %fusion.26, s32[1024]{0:T(1024)S(1)} %pad_clamp_fusion.2), kind=kCustom, calls=%fused_computation.clone | custom fusion | bytes 33554560 | tf_op jit(solution)/shard_map/jit(_take)/gather | solution.py:42
  518.9 14.2 %gather_fusion.3 = f32[32,512,256]{2,1,0:T(8,128)} fusion(f32[32,512,256]{2,1,0:T(8,128)} %fusion.24, s32[1024]{0:T(1024)S(1)} %pad_clamp_fusion.2), kind=kCustom, calls=%fused_computation.3.clone | custom fusion | bytes 33554560 | tf_op jit(solution)/shard_map/jit(_take)/gather | solution.py:42
  533.1 14.2 %gather_fusion.6 = f32[32,512,256]{2,1,0:T(8,128)} fusion(f32[32,512,256]{2,1,0:T(8,128)} %fusion.22, s32[1024]{0:T(1024)S(1)} %pad_clamp_fusion.2), kind=kCustom, calls=%fused_computation.6.clone | custom fusion | bytes 33554560 | tf_op jit(solution)/shard_map/jit(_take)/gather | solution.py:42
  547.2 14.3 %gather_fusion.9 = f32[32,512,256]{2,1,0:T(8,128)} fusion(f32[32,512,256]{2,1,0:T(8,128)} %fusion.20, s32[1024]{0:T(1024)S(1)} %pad_clamp_fusion.2), kind=kCustom, calls=%fused_computation.9.clone | custom fusion | bytes 33554560 | tf_op jit(solution)/shard_map/jit(_take)/gather | solution.py:42
  561.6 81.0 %fusion.6 = (f32[512,256]{1,0:T(8,128)S(1)}, f32[512,256]{1,0:T(8,128)S(1)}, f32[512,256]{1,0:T(8,128)}, f32[512,256]{1,0:T(8,128)}, f32[512,256]{1,0:T(8,128)},...) fusion(f32[32,512,256]{2,1,0:T(8,128)} %gather_fusion.9, ...), kind=kOutput, calls=%fused_computation.25 | convolution fusion | flops 1229455360 | bytes 264257632 | tf_op jit(solution)/shard_map/kri,kci->krc/dot_general | solution.py:15
  (52 shorter events, 39.7 us)
Async XLA Ops:
  6.5 98.4 %copy-start.6 = (bf16[4,256]{1,0:T(4,128)(2,1)S(1)}, bf16[4,256]{1,0:T(4,128)(2,1)}, u32[]{:S(2)}) copy-start(bf16[4,256]{1,0:T(4,128)(2,1)} %param.10) | copy-start | bytes 6148
  6.5 288.5 %copy-start.8 = (bf16[4,128]{1,0:T(4,128)(2,1)S(1)}, bf16[4,128]{1,0:T(4,128)(2,1)}, u32[]{:S(2)}) copy-start(bf16[4,128]{1,0:T(4,128)(2,1)} %param.9) | copy-start | bytes 3076
  6.5 296.9 %copy-start.7 = (s32[3,32]{1,0:T(4,128)S(1)}, s32[3,32]{1,0:T(4,128)}, u32[]{:S(2)}) copy-start(s32[3,32]{1,0:T(4,128)} %param.11) | copy-start | bytes 1156
  6.5 38.8 %all-gather.9.cloned.1.call-start = ((), (), s32[]{:S(2)}) async-start(), calls=%async_computation.3 | async-start | bytes 2621440 | tf_op jit(solution)/shard_map/all_gather | solution.py:22
  8.9 90.9 %all-gather.13.cloned.1.call-start = ((), (), s32[]{:S(2)}) async-start(), calls=%async_computation.5 | async-start | bytes 5242880 | tf_op jit(solution)/shard_map/all_gather | solution.py:23
  11.9 297.3 %all-gather.7.cloned.1.call-start = ((), (), s32[]{:S(2)}) async-start(), calls=%async_computation.2 | async-start | bytes 4718592 | tf_op jit(solution)/shard_map/all_gather | solution.py:30
  12.7 328.2 %all-gather.11.cloned.1.call-start = ((), (), s32[]{:S(2)}) async-start(), calls=%async_computation.4 | async-start | bytes 9437184 | tf_op jit(solution)/shard_map/all_gather | solution.py:31
  45.3 54.4 %all-to-all-start = ((bf16[4,2048,128]{2,0,1:T(4,128)(2,1)}), bf16[4,2048,128]{2,0,1:T(4,128)(2,1)S(1)}, u32[]{:S(2)}, u32[]{:S(2)}) async-start(bf16[4,2048,128]{2,0,1:T(4,128)(2,1)} %all-gather.9.cloned.1.call-done), calls=%async_computation | async-start | bytes 4194304 | tf_op jit(solution)/shard_map/all_to_all | solution.py:26
  99.8 207.4 %copy-start.1 = (bf16[4,2048,128]{2,0,1:T(4,128)(2,1)}, bf16[4,2048,128]{2,0,1:T(4,128)(2,1)S(1)}, u32[]{:S(2)}) copy-start(bf16[4,2048,128]{2,0,1:T(4,128)(2,1)S(1)} %all-to-all-done) | copy-start | bytes 6291460
  99.8 236.0 %all-to-all-start.1 = ((bf16[4,2048,256]{2,0,1:T(4,128)(2,1)}), bf16[4,2048,256]{2,0,1:T(4,128)(2,1)}, u32[]{:S(2)}, u32[]{:S(2)}) async-start(bf16[4,2048,256]{2,0,1:T(4,128)(2,1)} %all-gather.13.cloned.1.call-done), calls=%async_computation.1 | async-start | bytes 8388608 | tf_op jit(solution)/shard_map/all_to_all | solution.py:27
  309.3 10.4 %copy-start = (bf16[32,512,128]{2,1,0:T(8,128)(2,1)S(1)}, bf16[32,512,128]{2,1,0:T(8,128)(2,1)}, u32[]{:S(2)}) copy-start(bf16[32,512,128]{2,1,0:T(8,128)(2,1)} %all-gather.7.cloned.1.call-done) | copy-start | bytes 12582916
  547.2 14.3 %copy-start.2 = (f32[4,8,128]{2,1,0:T(8,128)S(1)}, f32[4,8,128]{2,1,0:T(8,128)}, u32[]{:S(2)}) copy-start(f32[4,8,128]{2,1,0:T(8,128)} %get-tuple-element.58) | copy-start | bytes 49156
  547.2 14.3 %copy-start.3 = (pred[32]{0:T(512)(128)(4,1)S(1)}, pred[32]{0:T(512)(128)(4,1)}, u32[]{:S(2)}) copy-start(pred[32]{0:T(512)(128)(4,1)} %get-tuple-element.27) | copy-start | bytes 100
  547.2 14.4 %copy-start.4 = (pred[32]{0:T(512)(128)(4,1)S(1)}, pred[32]{0:T(512)(128)(4,1)}, u32[]{:S(2)}) copy-start(pred[32]{0:T(512)(128)(4,1)} %get-tuple-element.41) | copy-start | bytes 100
  547.2 14.4 %copy-start.5 = (pred[32]{0:T(512)(128)(4,1)S(1)}, pred[32]{0:T(512)(128)(4,1)}, u32[]{:S(2)}) copy-start(pred[32]{0:T(512)(128)(4,1)} %get-tuple-element.43) | copy-start | bytes 100
Sparse Core Ops, SparseCore 0:
  9.2 36.1 all-gather.8
  47.2 52.5 all-gather.12
  101.4 87.5 all-gather.6
  190.5 108.7 all-gather.10
where the time goes:
time: 667 us; the launch traced here: 658 us
  blocking collectives  195 us (29%)
  local copies, waits for them, and re-layouts  183 us (27%)
  matrix products  158 us (24%)
  waiting for transfers between devices  82.7 us (12%)
  other arithmetic  14.9 us (2%)
  between operations  13.5 us (2%)
  starting transfers between devices  10.3 us (2%)
    all_gather x1, blocking collectives, on_device(): lax.all_gather(virt_gap, 'kpt', axis=0, tiled=True)  187 us
    gather x12, local copies, waits for them, and re-layouts, on_device(): virt_green = jnp.take(every_green, partner[transfer], axis=0)  170 us
    dot_general x8, matrix products, greens(): jnp.einsum('kri,kci->krc', row_panel, column_panel, preferred_element_typ...  158 us
    all_gather x1, waiting for transfers between devices, on_device(): lax.all_gather(virt_orbitals, 'row', axis=1, tiled=True)  49.3 us
    all_gather x1, waiting for transfers between devices, on_device(): lax.all_gather(occ_orbitals, 'row', axis=1, tiled=True)  32.1 us
  transfers between devices with their start and end apart: 6, of which 2 were waited for; matrix products, arithmetic and copies ran while one was open for 7% of the time, Pallas kernels for 0%

commit v1 on v0

v1 whole, which is shorter than its diff:
```python
import functools

import jax
import jax.numpy as jnp
from jax import lax
from jax.experimental import pallas as pl
from jax.experimental.pallas import tpu as pltpu
from jax.sharding import PartitionSpec as P

NTAU = 4
PAD = 16
SUB = 32


def kernel(nk, nr, per, occ_ref, virt_ref, gap_ref, partner_ref, out_ref, rows, cols, og, vg,
           local_sem, row_recv, col_recv, right_send, left_send, sib_send, col_send):
    K = nk * per
    npts, nocc = occ_ref.shape[1], occ_ref.shape[2]
    nall = rows.shape[2]
    ncol = cols.shape[1]
    tile = og.shape[1]
    j = lax.axis_index("kpt")
    i = lax.axis_index("row")
    c, s = j // 2, j % 2
    nc = nk // 2
    cpr = nk // nr
    root = j // cpr
    off = pl.multiple_of((j % cpr) * ncol, ncol)
    transfers = partner_ref.shape[0]

    def place(index):
        return jnp.where(index % 2 == 0, index // 2, nr - 1 - index // 2)

    def at_place(p):
        return jnp.where(p < nr // 2, 2 * p, 2 * (nr - 1 - p) + 1)

    me, top = place(i), place(root)
    ahead, behind = at_place((me + 1) % nr), at_place((me + nr - 1) % nr)
    dist_a, dist_b = (me - top + nr) % nr, (top - me + nr) % nr
    is_root = i == root
    has_right, has_left = c + 1 < nc, c > 0

    locals_ = []
    for a in range(per):
        m = j * per + a
        locals_.append((
            pltpu.make_async_copy(occ_ref.at[a], rows.at[m, pl.ds(0, npts), pl.ds(0, nocc)], local_sem.at[a, 0]),
            pltpu.make_async_copy(virt_ref.at[a], rows.at[m, pl.ds(0, npts), pl.ds(nocc, nall - nocc)], local_sem.at[a, 1]),
            pltpu.make_async_copy(gap_ref.at[a], rows.at[m, pl.ds(npts, PAD)], local_sem.at[a, 2]),
        ))
    for group in locals_:
        for copy in group:
            copy.start()

    barrier = pltpu.get_barrier_semaphore()

    def greet(device):
        pl.semaphore_signal(barrier, inc=1, device_id=device, device_id_type=pl.DeviceIdType.MESH)

    greet((j + 1 - 2 * s, i))
    greet((j, ahead))
    greet((j, behind))

    @pl.when(has_right)
    def _():
        greet((j + 2, i))

    @pl.when(has_left)
    def _():
        greet((j - 2, i))

    pl.semaphore_wait(barrier, 3 + has_right.astype(jnp.int32) + has_left.astype(jnp.int32))

    for group in locals_:
        for copy in group:
            copy.wait()

    def remote(src, dst, send, recv, device):
        return pltpu.make_async_remote_copy(src_ref=src, dst_ref=dst, send_sem=send, recv_sem=recv,
                                            device_id=device, device_id_type=pl.DeviceIdType.MESH)

    def to_right(m):
        return remote(rows.at[m], rows.at[m], right_send.at[m], row_recv.at[m], (j + 2, i))

    def to_left(m):
        return remote(rows.at[m], rows.at[m], left_send.at[m], row_recv.at[m], (j - 2, i))

    def to_sib(m):
        return remote(rows.at[m], rows.at[m], sib_send.at[m], row_recv.at[m], (j + 1 - 2 * s, i))

    def col_copy(m, device, from_root):
        src = rows.at[m, pl.ds(off, ncol)] if from_root else cols.at[m]
        return remote(src, cols.at[m], col_send.at[m], col_recv.at[m], (j, device))

    def root_copy(m):
        return pltpu.make_async_copy(rows.at[m, pl.ds(off, ncol)], cols.at[m], col_recv.at[m])

    def wait_row(m):
        pltpu.make_async_copy(rows.at[m], rows.at[m], row_recv.at[m]).wait()

    def wait_col(m):
        pltpu.make_async_copy(cols.at[m], cols.at[m], col_recv.at[m]).wait()

    def root_send(m, start):
        @pl.when(is_root)
        def _():
            if start:
                root_copy(m).start()
            for parity, device in ((0, ahead), (1, behind)):
                @pl.when(m % 2 == parity)
                def _():
                    copy = col_copy(m, device, True)
                    copy.start() if start else copy.wait_send()

    def row_stage(f, start):
        h, a = f // per, f % per

        def go(copy):
            copy.start() if start else copy.wait_send()

        @pl.when(h == 0)
        def _():
            m = j * per + a

            @pl.when(has_right)
            def _():
                go(to_right(m))

            @pl.when(has_left)
            def _():
                go(to_left(m))

            go(to_sib(m))
            root_send(m, start)

        for left in (True, False):
            there = (c - h >= 0) if left else (c + h < nc)
            src = (c - h) if left else (c + h)
            onward = has_right if left else has_left

            @pl.when(there & (h > 0))
            def _():
                m = (2 * src + s) * per + a
                if start:
                    wait_row(m)

                @pl.when(onward)
                def _():
                    go(to_right(m) if left else to_left(m))

                go(to_sib(m))
                root_send(m, start)

        for left in (True, False):
            there = (c - h >= 0) if left else ((c + h < nc) & (h > 0))
            src = (c - h) if left else (c + h)

            @pl.when(there)
            def _():
                m = (2 * src + 1 - s) * per + a
                if start:
                    wait_row(m)
                root_send(m, start)

    def col_stage(f, start):
        h, a = f // per, f % per
        for left in (True, False):
            there = (c - h >= 0) if left else ((c + h < nc) & (h > 0))
            src = (c - h) if left else (c + h)
            for core in range(2):
                @pl.when(there & jnp.logical_not(is_root))
                def _():
                    m = (2 * src + core) * per + a
                    if start:
                        wait_col(m)
                    for parity, dist, device in ((0, dist_a, ahead), (1, dist_b, behind)):
                        @pl.when((m % 2 == parity) & (dist < nr - 1))
                        def _():
                            copy = col_copy(m, device, False)
                            copy.start() if start else copy.wait_send()

    total = nc * per

    def step(f, carry):
        @pl.when(f < total)
        def _():
            row_stage(f, True)

        @pl.when(f > 0)
        def _():
            col_stage(f - 1, True)

        return carry

    lax.fori_loop(0, total + 1, step, 0)

    def root_done(m, carry):
        @pl.when(is_root)
        def _():
            wait_col(m)

        return carry

    lax.fori_loop(0, K, root_done, 0)

    tiles = npts // tile
    contract = (((1,), (1,)), ((), ()))

    def block(g, carry):
        t, r0 = g % NTAU, pl.multiple_of((g // NTAU) * tile, tile)
        moment = jnp.where(t == 0, 0.25, jnp.where(t == 1, 0.5, jnp.where(t == 2, 1.0, 2.0))).astype(jnp.float32)

        def one(k, inner):
            gap = rows[k, pl.ds(npts, PAD), :].astype(jnp.float32)
            factor = jnp.exp(-gap * moment)[0:1]
            panel = (rows[k, pl.ds(r0, tile), :].astype(jnp.float32) * factor).astype(jnp.bfloat16)
            column = cols[k]
            og[k] = lax.dot_general(panel[:, :nocc], column[:, :nocc], contract, preferred_element_type=jnp.float32)
            vg[k] = lax.dot_general(panel[:, nocc:], column[:, nocc:], contract, preferred_element_type=jnp.float32)
            return inner

        lax.fori_loop(0, K, one, 0, unroll=2)

        def piece(p, inner):
            here = pl.ds(pl.multiple_of(p * SUB, SUB), SUB)

            def add(k, sums):
                occ = og[k, here, :]
                return tuple(x + occ * vg[partner_ref[q, k], here, :] for q, x in enumerate(sums))

            zero = jnp.zeros((SUB, ncol), jnp.float32)
            sums = lax.fori_loop(0, K, add, (zero,) * transfers, unroll=4)
            for q in range(transfers):
                out_ref[q, t, pl.ds(pl.multiple_of(r0 + p * SUB, SUB), SUB), :] = sums[q]
            return inner

        lax.fori_loop(0, tile // SUB, piece, 0)
        return carry

    lax.fori_loop(0, tiles * NTAU, block, 0)

    def finish(f, carry):
        row_stage(f, False)
        col_stage(f, False)
        return carry

    lax.fori_loop(0, total, finish, 0)


def on_device(nk, nr, occ_orbitals, virt_orbitals, occ_gap, virt_gap, partner):
    per, npts, nocc = occ_orbitals.shape
    nv = virt_orbitals.shape[2]
    K, ncol, nall = nk * per, npts * nr // nk, nocc + nv
    tile = min(256, npts)
    transfers = partner.shape[0]
    gaps = jnp.broadcast_to(jnp.concatenate([occ_gap, virt_gap], axis=1)[:, None, :], (per, PAD, nall))
    dma = pltpu.SemaphoreType.DMA
    return pl.pallas_call(
        functools.partial(kernel, nk, nr, per),
        out_shape=jax.ShapeDtypeStruct((transfers, NTAU, npts, ncol), jnp.float32),
        in_specs=[pl.BlockSpec(memory_space=pl.ANY)] * 3 + [pl.BlockSpec(memory_space=pltpu.SMEM)],
        out_specs=pl.BlockSpec(memory_space=pltpu.VMEM),
        scratch_shapes=[
            pltpu.VMEM((K, npts + PAD, nall), jnp.bfloat16),
            pltpu.VMEM((K, ncol, nall), jnp.bfloat16),
            pltpu.VMEM((K, tile, ncol), jnp.float32),
            pltpu.VMEM((K, tile, ncol), jnp.float32),
            dma((per, 3)), dma((K,)), dma((K,)), dma((K,)), dma((K,)), dma((K,)), dma((K,)),
        ],
        compiler_params=pltpu.CompilerParams(
            collective_id=0, has_side_effects=True, vmem_limit_bytes=60 * 2**20),
    )(occ_orbitals, virt_orbitals, gaps, partner)


def solution(mesh):
    in_specs = (P("kpt", "row", None), P("kpt", "row", None), P("kpt", None), P("kpt", None), P())
    out_specs = P(None, None, "row", "kpt")
    return jax.shard_map(
        functools.partial(on_device, mesh.shape["kpt"], mesh.shape["row"]),
        mesh=mesh, in_specs=in_specs, out_specs=out_specs, check_vma=False,
    )
```

time: 667 us -> 366 us (0.55); the launches traced: 658 us -> 366 us
  Pallas kernels: 0 us -> 358 us
  blocking collectives: 195 us -> 0 us
  local copies, waits for them, and re-layouts: 183 us -> 6.52 us
  matrix products: 158 us -> 0 us
  waiting for transfers between devices: 82.7 us -> 0 us
  other arithmetic: 14.9 us -> 0.7 us
  between operations: 13.5 us -> 0.01 us
  starting transfers between devices: 10.3 us -> 0 us
    pallas_call x0 -> x1, Pallas kernels: none -> 358 us  [on_device(): pl.pallas_call(functools.partial(kernel, nk, nr, per), out_shape=jax.Shap...]
    all_gather x2 -> x0, blocking collectives: 195 us -> none  [the longest x1 187 us: on_device(): lax.all_gather(virt_gap, 'kpt', axis=0, tiled=True)]
    gather x12 -> x0, local copies, waits for them, and re-layouts: 170 us -> none  [on_device(): virt_green = jnp.take(every_green, partner[transfer], axis=0)]
    dot_general x8 -> x0, matrix products: 158 us -> none  [greens(): jnp.einsum('kri,kci->krc', row_panel, column_panel, preferred_element_typ...]
    all_gather x4 -> x0, waiting for transfers between devices: 81.5 us -> none  [the longest x1 49.3 us: on_device(): lax.all_gather(virt_orbitals, 'row', axis=1, tiled=True)]
    all_to_all x2 -> x0, starting transfers between devices: 10.2 us -> none  [the longest x1 5.1 us: on_device(): lax.all_to_all(virt_points, 'kpt', split_axis=1, concat_axis=0, tiled=True)]
    another operation x5 -> x0, other arithmetic: 8.66 us -> none  [on_device(): return jnp.stack(blocks, axis=1)]
    all_to_all x2 -> x0, local copies, waits for them, and re-layouts: 7.09 us -> none  [the longest x1 4.99 us: on_device(): lax.all_to_all(virt_points, 'kpt', split_axis=1, concat_axis=0, tiled=True)]
  transfers between devices with their start and end apart: 6 -> 0, of which waited for: 2 -> 0; matrix products, arithmetic and copies ran while one was open for 7% -> 0% of each run, Pallas kernels for 0% -> 0%
where the time goes in v1:
time: 366 us
  Pallas kernels  358 us (98%)
  local copies, waits for them, and re-layouts  6.52 us (2%)
    pallas_call x1, Pallas kernels, on_device(): pl.pallas_call(functools.partial(kernel, nk, nr, per), out_shape=jax.Shap...  358 us

profile of v1, /device:TPU:26, one launch (start us, length us, event | category | flops | bytes accessed | tf_op | source)
XLA Modules:
  0.0 365.7 jit_solution(7381978760173624025)
XLA Ops:
  0.0 0.7 pad_maximum_fusion
  0.7 0.6 broadcast_in_dim.2.gap_ref
  1.3 358.4 %shard_map.55 = f32[3,4,512,256]{3,2,1,0:T(8,128)} custom-call(bf16[4,512,128]{2,1,0:T(8,128)(2,1)} %occ_ref.1, bf16[4,512,256]{2,1,0:T(8,128)(2,1)} %virt_ref.1, bf16[4,16,384]{2,1,0:T(8,128)(2,1)} %broadcast_in_dim.2.gap_ref, s32[3,32]{1,0:T(4,128)} %partner_ref.1), custom_call_target="tpu_custom_call" | custom-call | tf_op jit(solution)/shard_map/pallas_call | solution.py:258
  359.8 5.9 %copy.7 = f32[3,4,512,256]{3,2,1,0:T(8,128)} copy(f32[3,4,512,256]{3,2,1,0:T(8,128)} %shard_map.55) | data formatting | bytes 12582912

commit v2 on v1

--- a/solution.py
+++ b/solution.py
@@ -10,6 +10,7 @@
 NTAU = 4
 PAD = 16
 SUB = 32
+LAG = 1
 
 
 def kernel(nk, nr, per, occ_ref, virt_ref, gap_ref, partner_ref, out_ref, rows, cols, og, vg,
@@ -101,13 +102,16 @@
     def wait_col(m):
         pltpu.make_async_copy(cols.at[m], cols.at[m], col_recv.at[m]).wait()
 
+    def way(m):
+        return (m + m // per) % 2
+
     def root_send(m, start):
         @pl.when(is_root)
         def _():
             if start:
                 root_copy(m).start()
             for parity, device in ((0, ahead), (1, behind)):
-                @pl.when(m % 2 == parity)
+                @pl.when(way(m) == parity)
                 def _():
                     copy = col_copy(m, device, True)
                     copy.start() if start else copy.wait_send()
@@ -162,46 +166,49 @@
                     wait_row(m)
                 root_send(m, start)
 
-    def col_stage(f, start):
+    def col_stage(f, start, parity, dist, device):
         h, a = f // per, f % per
         for left in (True, False):
             there = (c - h >= 0) if left else ((c + h < nc) & (h > 0))
             src = (c - h) if left else (c + h)
             for core in range(2):
-                @pl.when(there & jnp.logical_not(is_root))
+                m = (2 * src + core) * per + a
+
+                @pl.when(there & (way(m) == parity) & (dist > 0) & (dist < nr - 1))
                 def _():
-                    m = (2 * src + core) * per + a
                     if start:
                         wait_col(m)
-                    for parity, dist, device in ((0, dist_a, ahead), (1, dist_b, behind)):
-                        @pl.when((m % 2 == parity) & (dist < nr - 1))
-                        def _():
-                            copy = col_copy(m, device, False)
-                            copy.start() if start else copy.wait_send()
+                    copy = col_copy(m, device, False)
+                    copy.start() if start else copy.wait_send()
 
     total = nc * per
+    ways = ((0, dist_a, ahead), (1, dist_b, behind))
 
     def step(f, carry):
         @pl.when(f < total)
         def _():
             row_stage(f, True)
 
-        @pl.when(f > 0)
-        def _():
-            col_stage(f - 1, True)
-
-        return carry
-
-    lax.fori_loop(0, total + 1, step, 0)
-
-    def root_done(m, carry):
-        @pl.when(is_root)
-        def _():
-            wait_col(m)
-
-        return carry
-
-    lax.fori_loop(0, K, root_done, 0)
+        for parity, dist, device in ways:
+            then = f - LAG * dist
+
+            @pl.when((then >= 0) & (then < total))
+            def _():
+                col_stage(then, True, parity, dist, device)
+
+        return carry
+
+    lax.fori_loop(0, total + LAG * (nr - 2), step, 0)
+
+    def col_done(m, carry):
+        for parity, dist, _ in ways:
+            @pl.when((way(m) == parity) & ((dist == 0) | (dist == nr - 1)))
+            def _():
+                wait_col(m)
+
+        return carry
+
+    lax.fori_loop(0, K, col_done, 0)
 
     tiles = npts // tile
     contract = (((1,), (1,)), ((), ()))
@@ -241,7 +248,8 @@
 
     def finish(f, carry):
         row_stage(f, False)
-        col_stage(f, False)
+        for parity, dist, device in ways:
+            col_stage(f, False, parity, dist, device)
         return carry
 
     lax.fori_loop(0, total, finish, 0)

time: 366 us -> 202 us (0.55)
  Pallas kernels: 358 us -> 195 us
    pallas_call x1, Pallas kernels: 358 us -> 195 us  [on_device(): pl.pallas_call(functools.partial(kernel, nk, nr, per), out_shape=jax.Shap...]
where the time goes in v2:
time: 202 us
  Pallas kernels  195 us (97%)
  local copies, waits for them, and re-layouts  6.52 us (3%)
    pallas_call x1, Pallas kernels, on_device(): pl.pallas_call(functools.partial(kernel, nk, nr, per), out_shape=jax.Shap...  195 us
    unnamed x1, local copies, waits for them, and re-layouts  5.89 us

profile of v2, /device:TPU:26, one launch (start us, length us, event | category | flops | bytes accessed | tf_op | source)
XLA Modules:
  0.0 202.1 jit_solution(3121330137682857495)
XLA Ops:
  0.0 0.7 pad_maximum_fusion
  0.7 0.6 broadcast_in_dim.2.gap_ref
  1.3 194.8 %shard_map.55 = f32[3,4,512,256]{3,2,1,0:T(8,128)} custom-call(bf16[4,512,128]{2,1,0:T(8,128)(2,1)} %occ_ref.1, bf16[4,512,256]{2,1,0:T(8,128)(2,1)} %virt_ref.1, bf16[4,16,384]{2,1,0:T(8,128)(2,1)} %broadcast_in_dim.2.gap_ref, s32[3,32]{1,0:T(4,128)} %partner_ref.1), custom_call_target="tpu_custom_call" | custom-call | tf_op jit(solution)/shard_map/pallas_call | solution.py:266
  196.2 5.9 %copy.7 = f32[3,4,512,256]{3,2,1,0:T(8,128)} copy(f32[3,4,512,256]{3,2,1,0:T(8,128)} %shard_map.55) | data formatting | bytes 12582912

commit v3 on v2

--- a/solution.py
+++ b/solution.py
@@ -19,7 +19,6 @@
     npts, nocc = occ_ref.shape[1], occ_ref.shape[2]
     nall = rows.shape[2]
     ncol = cols.shape[1]
-    tile = og.shape[1]
     j = lax.axis_index("kpt")
     i = lax.axis_index("row")
     c, s = j // 2, j % 2
@@ -166,6 +165,27 @@
                     wait_row(m)
                 root_send(m, start)
 
+    contract = (((1,), (1,)), ((), ()))
+
+    def green(k, moment):
+        gap = rows[k, pl.ds(npts, PAD), :].astype(jnp.float32)[0:1]
+        factor = jnp.exp(-gap * moment)
+        panel = (rows[k, pl.ds(0, npts), :].astype(jnp.float32) * factor).astype(jnp.bfloat16)
+        column = cols[k]
+        og[k] = lax.dot_general(panel[:, :nocc], column[:, :nocc], contract, preferred_element_type=jnp.float32)
+        vg[k] = lax.dot_general(panel[:, nocc:], column[:, nocc:], contract, preferred_element_type=jnp.float32)
+
+    def green_stage(f):
+        h, a = f // per, f % per
+        for left in (True, False):
+            there = (c - h >= 0) if left else ((c + h < nc) & (h > 0))
+            src = (c - h) if left else (c + h)
+
+            @pl.when(there)
+            def _():
+                for core in range(2):
+                    green((2 * src + core) * per + a, 0.25)
+
     def col_stage(f, start, parity, dist, device):
         h, a = f // per, f % per
         for left in (True, False):
@@ -174,12 +194,15 @@
             for core in range(2):
                 m = (2 * src + core) * per + a
 
-                @pl.when(there & (way(m) == parity) & (dist > 0) & (dist < nr - 1))
+                @pl.when(there & (way(m) == parity))
                 def _():
                     if start:
                         wait_col(m)
-                    copy = col_copy(m, device, False)
-                    copy.start() if start else copy.wait_send()
+
+                    @pl.when((dist > 0) & (dist < nr - 1))
+                    def _():
+                        copy = col_copy(m, device, False)
+                        copy.start() if start else copy.wait_send()
 
     total = nc * per
     ways = ((0, dist_a, ahead), (1, dist_b, behind))
@@ -190,43 +213,32 @@
             row_stage(f, True)
 
         for parity, dist, device in ways:
-            then = f - LAG * dist
+            then = f - LAG * jnp.maximum(dist, 1)
 
             @pl.when((then >= 0) & (then < total))
             def _():
                 col_stage(then, True, parity, dist, device)
 
+        ready = f - LAG * (nr - 1)
+
+        @pl.when(ready >= 0)
+        def _():
+            green_stage(ready)
+
         return carry
 
-    lax.fori_loop(0, total + LAG * (nr - 2), step, 0)
-
-    def col_done(m, carry):
-        for parity, dist, _ in ways:
-            @pl.when((way(m) == parity) & ((dist == 0) | (dist == nr - 1)))
-            def _():
-                wait_col(m)
-
-        return carry
-
-    lax.fori_loop(0, K, col_done, 0)
-
-    tiles = npts // tile
-    contract = (((1,), (1,)), ((), ()))
-
-    def block(g, carry):
-        t, r0 = g % NTAU, pl.multiple_of((g // NTAU) * tile, tile)
-        moment = jnp.where(t == 0, 0.25, jnp.where(t == 1, 0.5, jnp.where(t == 2, 1.0, 2.0))).astype(jnp.float32)
-
-        def one(k, inner):
-            gap = rows[k, pl.ds(npts, PAD), :].astype(jnp.float32)
-            factor = jnp.exp(-gap * moment)[0:1]
-            panel = (rows[k, pl.ds(r0, tile), :].astype(jnp.float32) * factor).astype(jnp.bfloat16)
-            column = cols[k]
-            og[k] = lax.dot_general(panel[:, :nocc], column[:, :nocc], contract, preferred_element_type=jnp.float32)
-            vg[k] = lax.dot_general(panel[:, nocc:], column[:, nocc:], contract, preferred_element_type=jnp.float32)
-            return inner
-
-        lax.fori_loop(0, K, one, 0, unroll=2)
+    lax.fori_loop(0, total + LAG * (nr - 1), step, 0)
+
+    def block(t, carry):
+        @pl.when(t > 0)
+        def _():
+            moment = jnp.where(t == 1, 0.5, jnp.where(t == 2, 1.0, 2.0)).astype(jnp.float32)
+
+            def one(k, inner):
+                green(k, moment)
+                return inner
+
+            lax.fori_loop(0, K, one, 0, unroll=8)
 
         def piece(p, inner):
             here = pl.ds(pl.multiple_of(p * SUB, SUB), SUB)
@@ -236,15 +248,15 @@
                 return tuple(x + occ * vg[partner_ref[q, k], here, :] for q, x in enumerate(sums))
 
             zero = jnp.zeros((SUB, ncol), jnp.float32)
-            sums = lax.fori_loop(0, K, add, (zero,) * transfers, unroll=4)
+            sums = lax.fori_loop(0, K, add, (zero,) * transfers, unroll=16)
             for q in range(transfers):
-                out_ref[q, t, pl.ds(pl.multiple_of(r0 + p * SUB, SUB), SUB), :] = sums[q]
+                out_ref[q, t, here, :] = sums[q]
             return inner
 
-        lax.fori_loop(0, tile // SUB, piece, 0)
+        lax.fori_loop(0, npts // SUB, piece, 0)
         return carry
 
-    lax.fori_loop(0, tiles * NTAU, block, 0)
+    lax.fori_loop(0, NTAU, block, 0)
 
     def finish(f, carry):
         row_stage(f, False)
@@ -259,7 +271,7 @@
     per, npts, nocc = occ_orbitals.shape
     nv = virt_orbitals.shape[2]
     K, ncol, nall = nk * per, npts * nr // nk, nocc + nv
-    tile = min(256, npts)
+    tile = npts
     transfers = partner.shape[0]
     gaps = jnp.broadcast_to(jnp.concatenate([occ_gap, virt_gap], axis=1)[:, None, :], (per, PAD, nall))
     dma = pltpu.SemaphoreType.DMA
@@ -276,7 +288,7 @@
             dma((per, 3)), dma((K,)), dma((K,)), dma((K,)), dma((K,)), dma((K,)), dma((K,)),
         ],
         compiler_params=pltpu.CompilerParams(
-            collective_id=0, has_side_effects=True, vmem_limit_bytes=60 * 2**20),
+            collective_id=0, has_side_effects=True, vmem_limit_bytes=62 * 2**20),
     )(occ_orbitals, virt_orbitals, gaps, partner)
 
 

time: 202 us -> 174 us (0.86)
  Pallas kernels: 195 us -> 165 us
    pallas_call x1, Pallas kernels: 195 us -> 165 us  [on_device(): pl.pallas_call(functools.partial(kernel, nk, nr, per), out_shape=jax.Shap...]
where the time goes in v3:
time: 174 us; the launch traced here: 172 us
  Pallas kernels  165 us (95%)
  local copies, waits for them, and re-layouts  6.52 us (4%)
    pallas_call x1, Pallas kernels, on_device(): pl.pallas_call(functools.partial(kernel, nk, nr, per), out_shape=jax.Shap...  165 us
    unnamed x1, local copies, waits for them, and re-layouts  5.89 us

profile of v3, /device:TPU:26, one launch (start us, length us, event | category | flops | bytes accessed | tf_op | source)
XLA Modules:
  0.0 172.2 jit_solution(17806542251321550094)
XLA Ops:
  0.0 0.7 pad_maximum_fusion
  0.7 0.6 broadcast_in_dim.2.gap_ref
  1.3 164.9 %shard_map.55 = f32[3,4,512,256]{3,2,1,0:T(8,128)} custom-call(bf16[4,512,128]{2,1,0:T(8,128)(2,1)} %occ_ref.1, bf16[4,512,256]{2,1,0:T(8,128)(2,1)} %virt_ref.1, bf16[4,16,384]{2,1,0:T(8,128)(2,1)} %broadcast_in_dim.2.gap_ref, s32[3,32]{1,0:T(4,128)} %partner_ref.1), custom_call_target="tpu_custom_call" | custom-call | tf_op jit(solution)/shard_map/pallas_call | solution.py:278
  166.3 5.9 %copy.7 = f32[3,4,512,256]{3,2,1,0:T(8,128)} copy(f32[3,4,512,256]{3,2,1,0:T(8,128)} %shard_map.55) | data formatting | bytes 12582912

commit v4 on v3

--- a/solution.py
+++ b/solution.py
@@ -13,7 +13,7 @@
 LAG = 1
 
 
-def kernel(nk, nr, per, occ_ref, virt_ref, gap_ref, partner_ref, out_ref, rows, cols, og, vg,
+def kernel(nk, nr, per, occ_ref, virt_ref, gap_ref, partner_ref, out_ref, rows, cols, og, vg, stage, out_sem,
            local_sem, row_recv, col_recv, right_send, left_send, sib_send, col_send):
     K = nk * per
     npts, nocc = occ_ref.shape[1], occ_ref.shape[2]
@@ -229,7 +229,14 @@
 
     lax.fori_loop(0, total + LAG * (nr - 1), step, 0)
 
+    def out_copy(t):
+        return pltpu.make_async_copy(stage.at[t % 2], out_ref.at[:, t], out_sem.at[t % 2])
+
     def block(t, carry):
+        @pl.when(t > 1)
+        def _():
+            out_copy(t - 2).wait()
+
         @pl.when(t > 0)
         def _():
             moment = jnp.where(t == 1, 0.5, jnp.where(t == 2, 1.0, 2.0)).astype(jnp.float32)
@@ -250,13 +257,16 @@
             zero = jnp.zeros((SUB, ncol), jnp.float32)
             sums = lax.fori_loop(0, K, add, (zero,) * transfers, unroll=16)
             for q in range(transfers):
-                out_ref[q, t, here, :] = sums[q]
+                stage[t % 2, q, here, :] = sums[q]
             return inner
 
         lax.fori_loop(0, npts // SUB, piece, 0)
+        out_copy(t).start()
         return carry
 
     lax.fori_loop(0, NTAU, block, 0)
+    for t in (NTAU - 2, NTAU - 1):
+        out_copy(t).wait()
 
     def finish(f, carry):
         row_stage(f, False)
@@ -279,12 +289,13 @@
         functools.partial(kernel, nk, nr, per),
         out_shape=jax.ShapeDtypeStruct((transfers, NTAU, npts, ncol), jnp.float32),
         in_specs=[pl.BlockSpec(memory_space=pl.ANY)] * 3 + [pl.BlockSpec(memory_space=pltpu.SMEM)],
-        out_specs=pl.BlockSpec(memory_space=pltpu.VMEM),
+        out_specs=pl.BlockSpec(memory_space=pl.ANY),
         scratch_shapes=[
             pltpu.VMEM((K, npts + PAD, nall), jnp.bfloat16),
             pltpu.VMEM((K, ncol, nall), jnp.bfloat16),
             pltpu.VMEM((K, tile, ncol), jnp.float32),
             pltpu.VMEM((K, tile, ncol), jnp.float32),
+            pltpu.VMEM((2, transfers, npts, ncol), jnp.float32), dma((2,)),
             dma((per, 3)), dma((K,)), dma((K,)), dma((K,)), dma((K,)), dma((K,)), dma((K,)),
         ],
         compiler_params=pltpu.CompilerParams(

time: 174 us -> 172 us (0.989)
  no operation moved by 1% of the time
where the time goes in v4:
time: 172 us; the launch traced here: 171 us
  Pallas kernels  164 us (95%)
  local copies, waits for them, and re-layouts  6.52 us (4%)
    pallas_call x1, Pallas kernels, on_device(): pl.pallas_call(functools.partial(kernel, nk, nr, per), out_shape=jax.Shap...  164 us
    unnamed x1, local copies, waits for them, and re-layouts  5.89 us

profile of v4, /device:TPU:26, one launch (start us, length us, event | category | flops | bytes accessed | tf_op | source)
XLA Modules:
  0.0 170.8 jit_solution(15140478116457578544)
XLA Ops:
  0.0 0.7 pad_maximum_fusion
  0.7 0.6 broadcast_in_dim.2.gap_ref
  1.3 163.6 %shard_map.55 = f32[3,4,512,256]{3,2,1,0:T(8,128)} custom-call(bf16[4,512,128]{2,1,0:T(8,128)(2,1)} %occ_ref.1, bf16[4,512,256]{2,1,0:T(8,128)(2,1)} %virt_ref.1, bf16[4,16,384]{2,1,0:T(8,128)(2,1)} %broadcast_in_dim.2.gap_ref, s32[3,32]{1,0:T(4,128)} %partner_ref.1), custom_call_target="tpu_custom_call" | custom-call | tf_op jit(solution)/shard_map/pallas_call | solution.py:288
  164.9 5.9 %copy.7 = f32[3,4,512,256]{3,2,1,0:T(8,128)} copy(f32[3,4,512,256]{3,2,1,0:T(8,128)} %shard_map.55) | data formatting | bytes 12582912
